TPU v7x, 32 devices: a whole 2x2x4 slice. The times are simulated.
32 devices in a mesh: dp: 4 (over y, core), space: 4 (over z), tensor: 2 (over x).
Axes of the slice: x: 2, y: 2, z: 4, core: 2. Of those that a mesh axis runs over, the one named last changes fastest.
Arguments:
- feature_map: bfloat16 [4, 32, 48, 1536], P('dp', 'space', None, 'tensor'), may hold values from -12 to 12
- conv_kernel: float32 [7, 7, 1536], replicated, may hold values from -6 to 6
- conv_bias: float32 [1536], replicated, may hold values from -4 to 4
- norm_gain: float32 [1536], replicated, may hold values from 0.1 to 1.9
- norm_bias: float32 [1536], replicated, may hold values from -3 to 3
- expand_weight: bfloat16 [1536, 6144], P(None, 'tensor'), may hold values from -0.21875 to 0.21875
- expand_bias: float32 [6144], P('tensor'), may hold values from -3 to 3
- project_weight: bfloat16 [6144, 1536], P('tensor'), may hold values from -0.109375 to 0.109375
- project_bias: float32 [1536], P('tensor'), may hold values from -3 to 3
- layer_scale: float32 [1536], P('tensor'), may hold values from 0.3 to 1.5
- cotangent: bfloat16 [4, 32, 48, 1536], P('dp', 'space', None, 'tensor'), may hold values from -6 to 6
Outputs:
- block_out: bfloat16 [4, 32, 48, 1536], P('dp', 'space', None, 'tensor')
- grad_input: bfloat16 [4, 32, 48, 1536], P('dp', 'space', None, 'tensor')
- grad_expand: float32 [1536, 6144], P(None, 'tensor')
- grad_project: float32 [6144, 1536], P('tensor')
- grad_kernel: float32 [7, 7, 1536], P(None, None, 'tensor')
All inputs are finite; a program needn't handle non-finite values.
Results may differ from a plain program's by a relative error of at most 0.0067.
Values may be sent and summed in bfloat16 or wider, within the bound.
A program may use at most 192 MiB of HBM per device.

v0:
```python
import jax
import jax.numpy as jnp
from jax import lax
from jax.sharding import PartitionSpec as P

EPSILON = 1e-06
INV_ROOT_TWO = 0.7071067811865476
INV_ROOT_TAU = 0.3989422804014327


def padded_2(block, sides, width):
    for axis, dim in sides:
        count = lax.axis_size(axis)
        forward = [(i, i + 1) for i in range(count - 1)]
        backward = [(target, source) for source, target in forward]
        low = lax.ppermute(
            lax.slice_in_dim(block, block.shape[dim] - width, None, axis=dim), axis, forward
        )
        high = lax.ppermute(lax.slice_in_dim(block, 0, width, axis=dim), axis, backward)
        block = jnp.concatenate([low, block, high], axis=dim)
    return block


def row_rims(block_data):
    return padded_2(block_data, (("space", 1),), 3)


def all_channels(block_data):
    return lax.all_gather(block_data, "tensor", axis=1, tiled=True)


def channel_total(stacked):
    return lax.psum(stacked, "tensor")


def partial_sums(term_rows):
    return lax.psum_scatter(term_rows, "tensor", scatter_dimension=1, tiled=True)


def depthwise(padded, tap_weights, row_count, col_count):
    widened = jnp.pad(padded.astype(jnp.float32), ((0, 0), (0, 0), (3, 3), (0, 0)))
    running = jnp.zeros((widened.shape[0], row_count, col_count, widened.shape[3]), jnp.float32)
    for tap_row in range(7):
        for tap_col in range(7):
            running = (
                running
                + tap_weights[tap_row, tap_col]
                * widened[:, tap_row : tap_row + row_count, tap_col : tap_col + col_count, :]
            )
    return running


def kernel_grad(grad_block, padded, row_count, col_count):
    widened = jnp.pad(padded.astype(jnp.float32), ((0, 0), (0, 0), (3, 3), (0, 0)))
    grad_float = grad_block.astype(jnp.float32)
    tap_rows = []
    for tap_row in range(7):
        tap_line = []
        for tap_col in range(7):
            window = widened[:, tap_row : tap_row + row_count, tap_col : tap_col + col_count, :]
            tap_line.append(jnp.sum(grad_float * window, axis=(0, 1, 2)))
        tap_rows.append(jnp.stack(tap_line))
    return jnp.stack(tap_rows)


def gelu_slope(values):
    cumulative = 0.5 * (1.0 + lax.erf(values * INV_ROOT_TWO))
    density = jnp.exp(-0.5 * values * values) * INV_ROOT_TAU
    return cumulative + values * density


def body(
    feature_map,
    conv_kernel,
    conv_bias,
    norm_gain,
    norm_bias,
    expand_weight,
    expand_bias,
    project_weight,
    project_bias,
    layer_scale,
    cotangent,
):
    images, row_count, col_count, shard_width = feature_map.shape
    pixels = images * row_count * col_count
    full_width = expand_weight.shape[0]
    offset = lax.axis_index("tensor") * shard_width
    own_gain = lax.dynamic_slice_in_dim(norm_gain, offset, shard_width, 0)
    own_kernel = lax.dynamic_slice_in_dim(conv_kernel, offset, shard_width, 2)
    padded = row_rims(feature_map)
    own_bias = lax.dynamic_slice_in_dim(conv_bias, offset, shard_width, 0)
    own_shift = lax.dynamic_slice_in_dim(norm_bias, offset, shard_width, 0)
    filtered = (depthwise(padded, own_kernel, row_count, col_count) + own_bias).reshape(
        pixels, shard_width
    )
    average = channel_total(jnp.sum(filtered, axis=1)) / full_width
    centered = filtered - average[:, None]
    spread = channel_total(jnp.sum(centered * centered, axis=1)) / full_width
    inverse = lax.rsqrt(spread + EPSILON)[:, None]
    unit_norm = centered * inverse
    gathered = all_channels((unit_norm * own_gain + own_shift).astype(jnp.bfloat16))
    hidden = jnp.dot(gathered, expand_weight, preferred_element_type=jnp.float32) + expand_bias
    activated = jax.nn.gelu(hidden, approximate=False).astype(jnp.bfloat16)
    projected = partial_sums(jnp.dot(activated, project_weight, preferred_element_type=jnp.float32))
    residual = feature_map.reshape(pixels, shard_width).astype(jnp.float32)
    block_out = (
        (residual + layer_scale * (projected + project_bias))
        .astype(jnp.bfloat16)
        .reshape(feature_map.shape)
    )
    grad_scaled = (cotangent.reshape(pixels, shard_width).astype(jnp.float32) * layer_scale).astype(
        jnp.bfloat16
    )
    grad_full = all_channels(grad_scaled)
    grad_project = lax.dot_general(
        activated, grad_full, (((0,), (0,)), ((), ())), preferred_element_type=jnp.float32
    )
    grad_act = lax.dot_general(
        grad_full, project_weight, (((1,), (1,)), ((), ())), preferred_element_type=jnp.float32
    )
    grad_hidden = (grad_act * gelu_slope(hidden)).astype(jnp.bfloat16)
    grad_expand = lax.dot_general(
        gathered, grad_hidden, (((0,), (0,)), ((), ())), preferred_element_type=jnp.float32
    )
    normed_terms = lax.dot_general(
        grad_hidden, expand_weight, (((1,), (1,)), ((), ())), preferred_element_type=jnp.float32
    )
    grad_normed = partial_sums(normed_terms)
    scaled_grad = grad_normed * own_gain
    channel_means = (
        lax.psum(
            jnp.stack([jnp.sum(scaled_grad, axis=1), jnp.sum(scaled_grad * unit_norm, axis=1)]),
            "tensor",
        )
        / full_width
    )
    grad_filtered = (
        (scaled_grad - channel_means[0][:, None] - unit_norm * channel_means[1][:, None]) * inverse
    ).astype(jnp.bfloat16)
    grad_block = grad_filtered.reshape(images, row_count, col_count, shard_width)
    grad_kernel = kernel_grad(grad_block, padded, row_count, col_count)
    grad_padded = row_rims(grad_block)
    grad_input = (
        cotangent.astype(jnp.float32)
        + depthwise(grad_padded, own_kernel[::-1, ::-1], row_count, col_count)
    ).astype(jnp.bfloat16)
    grad_expand, grad_project, grad_kernel = lax.psum(
        (grad_expand, grad_project, grad_kernel), ("dp", "space")
    )
    return (block_out, grad_input, grad_expand, grad_project, grad_kernel)


def solution(mesh):
    in_specs = (
        P("dp", "space", None, "tensor"),
        P(),
        P(),
        P(),
        P(),
        P(None, "tensor"),
        P("tensor"),
        P("tensor", None),
        P("tensor"),
        P("tensor"),
        P("dp", "space", None, "tensor"),
    )
    out_specs = (
        P("dp", "space", None, "tensor"),
        P("dp", "space", None, "tensor"),
        P(None, "tensor"),
        P("tensor", None),
        P(None, None, "tensor"),
    )
    return jax.shard_map(body, mesh=mesh, in_specs=in_specs, out_specs=out_specs, check_vma=False)
```

profile of v0, /device:TPU:0, one launch (start us, length us, event | category | flops | bytes accessed | tf_op | source)
XLA Modules:
  0.0 898.0 jit_solution(5840020140493676337)
XLA Ops:
  7.2 0.0 copy-start.3
  7.2 0.0 all-gather.3.cloned.1.call-start
  7.2 1.1 fusion.175
  8.4 5.0 collective-permute-start
  13.3 1.3 collective-permute-start.1
  14.6 0.8 dynamic_slice.14
  15.4 0.8 dynamic_slice.13
  16.2 0.8 dynamic_slice.15
  17.0 2.4 fusion.161
  19.4 2.7 collective-permute-done.1
  22.1 0.2 maximum_convert_fusion
  22.3 12.7 %fusion.173 = (f32[8,48]{1,0:T(8,128)S(1)}, f32[1,8,48,768]{3,2,1,0:T(8,128)S(1)}) fusion(f32[768]{0:T(1024)S(1)} %dynamic_slice.13, f32[768]{0:T(1024)S(1)} %get-tuple-element.104, f32[768]{0:T(1024)S(1)} %get-tuple-element.57, f32[768]{0:T(1024)S(1)} %get-tuple-element.58, f32[1,14,48,768]{3,2,1,0:T(8,128)S(1)} %maximum_convert_fusion, ...), kind=kLoop, calls=%fused_computation.396 | loop fusion | flops 29195904 | bytes 11707904 | tf_op jit(solution)/shard_map/reduce_sum | solution.py:97
  35.0 0.1 reduce_sum.482
  35.1 4.9 psum.42
  40.0 0.1 sub.30
  40.1 0.3 multiply_reduce_fusion.1
  40.4 0.1 reduce_sum.484
  40.4 4.9 psum.43
  45.4 1.1 add_convert_fusion
  46.4 0.0 all-gather.3.cloned.1.call-update
  46.5 0.0 reduce-scatter.3.cloned.1.call-start
  46.5 23.1 %all-gather.3.cloned.1.call-done = bf16[384,1536]{1,0:T(8,128)(2,1)} async-done(((bf16[384,768]{1,0:T(8,128)(2,1)}), bf16[384,1536]{1,0:T(8,128)(2,1)}) %all-gather.3.cloned.1.call-update) | async-done | bytes 1179664 | tf_op jit(solution)/shard_map/all_gather | solution.py:29
  69.6 17.0 %fusion.2 = (bf16[384,3072]{1,0:T(8,128)(2,1)S(1)}, f32[384,3072]{1,0:T(8,128)}) fusion(f32[3072]{0:T(1024)S(1)} %copy-done.13, bf16[384,1536]{1,0:T(8,128)(2,1)} %all-gather.3.cloned.1.call-done, bf16[1536,3072]{1,0:T(8,128)(2,1)} %param.16), kind=kOutput, calls=%fused_computation.53 | convolution fusion | flops 3701735424 | bytes 17707008 | tf_op jit(solution)/shard_map/dot_general | solution.py:103
  86.6 1.4 copy-done.4
  88.0 7.7 fusion.176
  95.7 0.0 reduce-scatter.3.cloned.1.call-update
  95.7 0.0 all-gather.5.cloned.1.call-start
  95.8 34.9 %reduce-scatter.3.cloned.1.call-done = f32[384,768]{1,0:T(8,128)} async-done(((f32[384,1536]{1,0:T(8,128)}), f32[384,768]{1,0:T(8,128)}) %reduce-scatter.3.cloned.1.call-update) | async-done | bytes 1179664 | tf_op jit(solution)/shard_map/reduce_scatter | solution.py:37
  130.7 2.9 fusion.158
  133.6 0.0 all-gather.5.cloned.1.call-update
  133.6 0.2 reduce-scatter.5.cloned.1.call-start
  133.8 22.7 %all-gather.5.cloned.1.call-done = bf16[384,1536]{1,0:T(8,128)(2,1)} async-done(((bf16[384,768]{1,0:T(8,128)(2,1)}), bf16[384,1536]{1,0:T(8,128)(2,1)}) %all-gather.5.cloned.1.call-update) | async-done | bytes 1179664 | tf_op jit(solution)/shard_map/all_gather | solution.py:29
  156.5 8.3 fusion.8
  164.8 0.0 copy-start.6
  164.8 1.4 copy-done.6
  166.2 7.8 fusion.177
  174.0 0.0 reduce-scatter.5.cloned.1.call-update
  174.0 0.0 all-reduce.5.cloned.1.call-start
  174.1 11.3 %fusion.178 = f32[1536,3072]{1,0:T(8,128)} fusion(bf16[384,1536]{1,0:T(8,128)(2,1)} %all-gather.3.cloned.1.call-done, bf16[384,3072]{1,0:T(8,128)(2,1)} %copy-done.6), kind=kOutput, calls=%fused_computation.401 | convolution fusion | flops 3623878656 | bytes 22413312 | tf_op jit(solution)/shard_map/dot_general | solution.py:123
  185.4 9.5 %fusion.179 = f32[3072,1536]{1,0:T(8,128)} fusion(bf16[384,3072]{1,0:T(8,128)(2,1)S(1)} %copy-done.5, bf16[384,1536]{1,0:T(8,128)(2,1)S(1)} %copy-done.8), kind=kOutput, calls=%fused_computation.402 | convolution fusion | flops 3623878656 | bytes 22413312 | tf_op jit(solution)/shard_map/dot_general | solution.py:116
  194.9 14.1 %reduce-scatter.5.cloned.1.call-done = f32[384,768]{1,0:T(8,128)} async-done(((f32[384,1536]{1,0:T(8,128)}), f32[384,768]{1,0:T(8,128)}) %reduce-scatter.5.cloned.1.call-update) | async-done | bytes 1179664 | tf_op jit(solution)/shard_map/reduce_scatter | solution.py:37
  209.0 1.7 multiply_reduce_fusion.2
  210.7 5.2 psum.44
  215.8 1.6 multiply_convert_fusion
  217.5 0.0 copy-start
  217.5 2.0 fusion.153
  219.5 2.9 fusion.155
  222.5 2.9 fusion.154
  226.4 0.0 copy-start.9
  226.4 0.6 copy-done.9
  227.1 0.0 all-reduce.5.cloned.1.call-update
  227.1 0.4 copy-done.1
  227.6 3.4 collective-permute-start.2
  231.0 0.0 copy-start.7
  231.0 1.4 collective-permute-start.3
  232.4 5.7 collective-permute-done.2
  238.1 6.5 collective-permute-done.3
  244.5 0.2 maximum_convert_fusion.1
  244.7 9.7 %fusion.104 = bf16[1,8,48,768]{3,2,1,0:T(8,128)(2,1)} fusion(f32[1,14,48,768]{3,2,1,0:T(8,128)S(1)} %maximum_convert_fusion.1, f32[768]{0:T(1024)S(1)} %get-tuple-element.104, f32[768]{0:T(1024)S(1)} %get-tuple-element.57, f32[768]{0:T(1024)S(1)} %get-tuple-element.58, f32[768]{0:T(1024)S(1)} %get-tuple-element.59, f32[768]{0:T(1024)S(1)} %get-tuple-element.60, ...), kind=kLoop, calls=%fused_computation.247 | loop fusion | flops 29491200 | bytes 11702272 | tf_op jit(solution)/shard_map/convert_element_type | solution.py:147
  254.4 610.9 %all-reduce.5.cloned.1.call-done = (f32[1536,3072]{1,0:T(8,128)}, f32[3072,1536]{1,0:T(8,128)}, f32[7,7,768]{2,1,0:T(8,128)}) async-done(((f32[1536,3072]{1,0:T(8,128)}, f32[3072,1536]{1,0:T(8,128)}, f32[7,7,768]{2,1,0:T(8,128)}), (f32[1536,3072]{1,0:T(8,128)}, f32[3072,1536]{1,0:T(8,128)}, f32[7,7,768]{2,1,0:T(8,128)})) %all-reduce.5.cloned.1.call-update) | async-done | bytes 37899280 | tf_op jit(solution)/shard_map/psum | solution.py:148
  865.3 15.4 %copy.25 = f32[1536,3072]{1,0:T(8,128)} copy(f32[1536,3072]{1,0:T(8,128)} %get-tuple-element.122) | data formatting | bytes 37748736
  880.7 3.2 copy-done.2
  883.9 6.8 copy.26
  890.8 0.7 copy.27
  (90 shorter events, 0.7 us)
Async XLA Ops:
  7.2 14.9 %copy-start.3 = (bf16[1,8,48,768]{3,2,1,0:T(8,128)(2,1)S(1)}, bf16[1,8,48,768]{3,2,1,0:T(8,128)(2,1)}, u32[]{:S(2)}) copy-start(bf16[1,8,48,768]{3,2,1,0:T(8,128)(2,1)} %param.11) | copy-start | bytes 1769476
  7.2 62.4 %all-gather.3.cloned.1.call-start = ((), (), s32[]{:S(2)}) async-start(), calls=%async_computation.2 | async-start | bytes 1769472 | tf_op jit(solution)/shard_map/all_gather | solution.py:29
  8.4 11.0 %collective-permute-start = (bf16[1,3,48,768]{3,2,1,0:T(8,128)(2,1)S(1)}, bf16[1,3,48,768]{3,2,1,0:T(8,128)(2,1)S(1)}, u32[]{:S(2)}, u32[]{:S(2)}) collective-permute-start(bf16[1,3,48,768]{3,2,1,0:T(8,128)(2,1)S(1)} %get-tuple-element.114), channel_id=1, source_target_pairs={{0,2},{2,4},{4,6},{1,3},{3,5},{5,7},{8,10},{10,12},{12,14},{9,11},... | collective-permute-start | bytes 663560 | tf_op jit(solution)/shard_map/ppermute | solution.py:16
  13.3 8.8 collective-permute-start.1
  45.4 24.2 %copy-start.13 = (f32[3072]{0:T(1024)S(1)}, f32[3072]{0:T(1024)}, u32[]{:S(2)}) copy-start(f32[3072]{0:T(1024)} %param.17) | copy-start | bytes 36868
  46.5 84.2 %reduce-scatter.3.cloned.1.call-start = ((), (), s32[]{:S(2)}) async-start(), calls=%async_computation.3 | async-start | bytes 3538944 | tf_op jit(solution)/shard_map/reduce_scatter | solution.py:37
  86.6 1.4 copy-start.4
  95.7 35.0 %copy-start.11 = (f32[768]{0:T(1024)S(1)}, f32[768]{0:T(1024)}, u32[]{:S(2)}) copy-start(f32[768]{0:T(1024)} %param.20) | copy-start | bytes 9220
  95.7 35.0 %copy-start.12 = (f32[768]{0:T(1024)S(1)}, f32[768]{0:T(1024)}, u32[]{:S(2)}) copy-start(f32[768]{0:T(1024)} %param.19) | copy-start | bytes 9220
  95.7 60.8 %all-gather.5.cloned.1.call-start = ((), (), s32[]{:S(2)}) async-start(), calls=%async_computation.4 | async-start | bytes 1769472 | tf_op jit(solution)/shard_map/all_gather | solution.py:29
  133.6 75.4 %reduce-scatter.5.cloned.1.call-start = ((), (), s32[]{:S(2)}) async-start(), calls=%async_computation.5 | async-start | bytes 3538944 | tf_op jit(solution)/shard_map/reduce_scatter | solution.py:37
  164.8 1.4 copy-start.6
  174.0 691.3 %all-reduce.5.cloned.1.call-start = ((), (), s32[]{:S(2)}) async-start(), calls=%async_computation.6 | async-start | bytes 75841536 | tf_op jit(solution)/shard_map/psum | solution.py:148
  174.1 11.3 %copy-start.5 = (bf16[384,3072]{1,0:T(8,128)(2,1)S(1)}, bf16[384,3072]{1,0:T(8,128)(2,1)}, u32[]{:S(2)}) copy-start(bf16[384,3072]{1,0:T(8,128)(2,1)} %copy-done.4) | copy-start | bytes 7077892
  174.1 11.3 %copy-start.8 = (bf16[384,1536]{1,0:T(8,128)(2,1)S(1)}, bf16[384,1536]{1,0:T(8,128)(2,1)}, u32[]{:S(2)}) copy-start(bf16[384,1536]{1,0:T(8,128)(2,1)} %all-gather.5.cloned.1.call-done) | copy-start | bytes 3538948
  217.5 5.0 copy-start
  226.4 0.7 copy-start.9
  226.4 1.1 copy-start.1
  227.6 10.5 %collective-permute-start.2 = (bf16[1,3,48,768]{3,2,1,0:T(8,128)(2,1)S(1)}, bf16[1,3,48,768]{3,2,1,0:T(8,128)(2,1)S(1)}, u32[]{:S(2)}, u32[]{:S(2)}) collective-permute-start(bf16[1,3,48,768]{3,2,1,0:T(8,128)(2,1)S(1)} %get-tuple-element.112), channel_id=1, source_target_pairs={{0,2},{2,4},{4,6},{1,3},{3,5},{5,7},{8,10},{10,12},{12,14},{9,11},... | collective-permute-start | bytes 663560 | tf_op jit(solution)/shard_map/ppermute | solution.py:16
  231.0 13.7 %copy-start.7 = (bf16[1,8,48,768]{3,2,1,0:T(8,128)(2,1)S(1)}, bf16[1,8,48,768]{3,2,1,0:T(8,128)(2,1)}, u32[]{:S(2)}) copy-start(bf16[1,8,48,768]{3,2,1,0:T(8,128)(2,1)} %param.21) | copy-start | bytes 1769476
  231.0 13.5 %collective-permute-start.3 = (bf16[1,3,48,768]{3,2,1,0:T(8,128)(2,1)S(1)}, bf16[1,3,48,768]{3,2,1,0:T(8,128)(2,1)S(1)}, u32[]{:S(2)}, u32[]{:S(2)}) collective-permute-start(bf16[1,3,48,768]{3,2,1,0:T(8,128)(2,1)S(1)} %get-tuple-element.113), channel_id=1, source_target_pairs={{2,0},{4,2},{6,4},{3,1},{5,3},{7,5},{10,8},{12,10},{14,12},{11,9},... | collective-permute-start | bytes 663560 | tf_op jit(solution)/shard_map/ppermute | solution.py:19
  865.3 18.6 %copy-start.2 = (f32[3072,1536]{1,0:T(8,128)S(1)}, f32[3072,1536]{1,0:T(8,128)}, u32[]{:S(2)}) copy-start(f32[3072,1536]{1,0:T(8,128)} %get-tuple-element.123) | copy-start | bytes 56623108
  883.9 6.9 copy-start.10
Sparse Core Ops, SparseCore 0:
  46.6 22.9 all-gather.2
  95.9 34.7 reduce-scatter.2
  133.7 22.7 all-gather.4
  174.1 34.7 reduce-scatter.4
  227.2 638.0 all-reduce.4
where the time goes:
time: 899 us; the launch traced here: 898 us
  waiting for transfers between devices  721 us (80%)
  matrix products  61.6 us (7%)
  other arithmetic  38.1 us (4%)
  local copies, waits for them, and re-layouts  36.8 us (4%)
  blocking collectives  15 us (2%)
  between operations  14.5 us (2%)
  starting transfers between devices  11.5 us (1%)
    psum x1, waiting for transfers between devices, body(): lax.psum((grad_expand, grad_project, grad_kernel), ('dp', 'space'))  611 us
    reduce_scatter x2, waiting for transfers between devices, partial_sums(): lax.psum_scatter(term_rows, 'tensor', scatter_dimension=1, tiled=True)  49 us
    all_gather x2, waiting for transfers between devices, all_channels(): return lax.all_gather(block_data, 'tensor', axis=1, tiled=True)  45.8 us
    unnamed x37, local copies, waits for them, and re-layouts  30.1 us
  transfers between devices with their start and end apart: 9, of which 8 were waited for; matrix products, arithmetic and copies ran while one was open for 4% of the time, Pallas kernels for 0%

commit v1 on v0

--- a/solution.py
+++ b/solution.py
@@ -35,6 +35,12 @@
 
 def partial_sums(term_rows):
     return lax.psum_scatter(term_rows, "tensor", scatter_dimension=1, tiled=True)
+
+
+def pixel_total(term, dim):
+    shared = lax.psum_scatter(term, ("dp", "space"), scatter_dimension=dim, tiled=True)
+    whole = lax.all_gather(shared.astype(jnp.bfloat16), ("dp", "space"), axis=dim, tiled=True)
+    return whole.astype(jnp.float32)
 
 
 def depthwise(padded, tap_weights, row_count, col_count):
@@ -113,15 +119,21 @@
         jnp.bfloat16
     )
     grad_full = all_channels(grad_scaled)
-    grad_project = lax.dot_general(
-        activated, grad_full, (((0,), (0,)), ((), ())), preferred_element_type=jnp.float32
+    grad_project = pixel_total(
+        lax.dot_general(
+            activated, grad_full, (((0,), (0,)), ((), ())), preferred_element_type=jnp.float32
+        ),
+        1,
     )
     grad_act = lax.dot_general(
         grad_full, project_weight, (((1,), (1,)), ((), ())), preferred_element_type=jnp.float32
     )
     grad_hidden = (grad_act * gelu_slope(hidden)).astype(jnp.bfloat16)
-    grad_expand = lax.dot_general(
-        gathered, grad_hidden, (((0,), (0,)), ((), ())), preferred_element_type=jnp.float32
+    grad_expand = pixel_total(
+        lax.dot_general(
+            gathered, grad_hidden, (((0,), (0,)), ((), ())), preferred_element_type=jnp.float32
+        ),
+        0,
     )
     normed_terms = lax.dot_general(
         grad_hidden, expand_weight, (((1,), (1,)), ((), ())), preferred_element_type=jnp.float32
@@ -145,9 +157,7 @@
         cotangent.astype(jnp.float32)
         + depthwise(grad_padded, own_kernel[::-1, ::-1], row_count, col_count)
     ).astype(jnp.bfloat16)
-    grad_expand, grad_project, grad_kernel = lax.psum(
-        (grad_expand, grad_project, grad_kernel), ("dp", "space")
-    )
+    grad_kernel = lax.psum(grad_kernel, ("dp", "space"))
     return (block_out, grad_input, grad_expand, grad_project, grad_kernel)
 
 

time: 899 us -> 875 us (0.973)
  waiting for transfers between devices: 721 us -> 683 us
  other arithmetic: 38.1 us -> 55.1 us
  local copies, waits for them, and re-layouts: 36.8 us -> 25.4 us
    psum x1, waiting for transfers between devices: 611 us -> 78.1 us  [body(): grad_kernel = lax.psum(grad_kernel, ('dp', 'space'))]
    reduce_scatter x0 -> x2, waiting for transfers between devices: none -> 363 us  [pixel_total(): lax.psum_scatter(term, ('dp', 'space'), scatter_dimension=dim, tiled=True)]
    all_gather x0 -> x2, waiting for transfers between devices: none -> 110 us  [pixel_total(): lax.all_gather(shared.astype(jnp.bfloat16), ('dp', 'space'), axis=dim, ti...]
    reduce_scatter x2, waiting for transfers between devices: 49 us -> 68.7 us  [partial_sums(): lax.psum_scatter(term_rows, 'tensor', scatter_dimension=1, tiled=True)]
    convert_element_type x0 -> x3, other arithmetic: none -> 17 us  [the longest x1 12.7 us: pixel_total(): return whole.astype(jnp.float32)]
    unnamed x37 -> x30, local copies, waits for them, and re-layouts: 30.1 us -> 18.7 us
  transfers between devices with their start and end apart: 9 -> 13, of which waited for: 8 -> 12; matrix products, arithmetic and copies ran while one was open for 4% -> 10% of each run, Pallas kernels for 0% -> 0%
where the time goes in v1:
time: 875 us; the launch traced here: 874 us
  waiting for transfers between devices  683 us (78%)
  matrix products  68.8 us (8%)
  other arithmetic  55.1 us (6%)
  local copies, waits for them, and re-layouts  25.4 us (3%)
  blocking collectives  15 us (2%)
  between operations  14.5 us (2%)
  starting transfers between devices  11.6 us (1%)
    reduce_scatter x2, waiting for transfers between devices, pixel_total(): lax.psum_scatter(term, ('dp', 'space'), scatter_dimension=dim, tiled=True)  363 us
    all_gather x2, waiting for transfers between devices, pixel_total(): lax.all_gather(shared.astype(jnp.bfloat16), ('dp', 'space'), axis=dim, ti...  110 us
    psum x1, waiting for transfers between devices, body(): grad_kernel = lax.psum(grad_kernel, ('dp', 'space'))  78.1 us
    reduce_scatter x2, waiting for transfers between devices, partial_sums(): lax.psum_scatter(term_rows, 'tensor', scatter_dimension=1, tiled=True)  68.7 us
    all_gather x2, waiting for transfers between devices, all_channels(): return lax.all_gather(block_data, 'tensor', axis=1, tiled=True)  45.8 us
    unnamed x30, local copies, waits for them, and re-layouts  18.7 us
  transfers between devices with their start and end apart: 13, of which 12 were waited for; matrix products, arithmetic and copies ran while one was open for 10% of the time, Pallas kernels for 0%

profile of v1, /device:TPU:0, one launch (start us, length us, event | category | flops | bytes accessed | tf_op | source)
XLA Modules:
  0.0 873.7 jit_solution(9765757772026388206)
XLA Ops:
  7.2 0.0 all-gather.5.cloned.1.call-start
  7.2 1.1 fusion.175
  8.4 5.0 collective-permute-start
  13.3 1.3 collective-permute-start.1
  14.6 0.8 dynamic_slice.14
  15.4 0.8 dynamic_slice.13
  16.2 0.8 dynamic_slice.15
  17.0 2.4 fusion.161
  19.4 2.7 collective-permute-done.1
  22.1 0.2 maximum_convert_fusion
  22.3 12.7 %fusion.173 = (f32[8,48]{1,0:T(8,128)S(1)}, f32[1,8,48,768]{3,2,1,0:T(8,128)S(1)}) fusion(f32[768]{0:T(1024)S(1)} %dynamic_slice.13, f32[768]{0:T(1024)S(1)} %get-tuple-element.109, f32[768]{0:T(1024)S(1)} %get-tuple-element.62, f32[768]{0:T(1024)S(1)} %get-tuple-element.63, f32[1,14,48,768]{3,2,1,0:T(8,128)S(1)} %maximum_convert_fusion, ...), kind=kLoop, calls=%fused_computation.396 | loop fusion | flops 29195904 | bytes 11707904 | tf_op jit(solution)/shard_map/reduce_sum | solution.py:103
  35.0 0.1 reduce_sum.482
  35.1 4.9 psum.28
  40.0 0.1 sub.30
  40.1 0.3 multiply_reduce_fusion.1
  40.4 0.1 reduce_sum.484
  40.4 4.9 psum.29
  45.4 1.1 add_convert_fusion
  46.4 0.0 all-gather.5.cloned.1.call-update
  46.5 0.0 reduce-scatter.5.cloned.1.call-start
  46.5 23.1 %all-gather.5.cloned.1.call-done = bf16[384,1536]{1,0:T(8,128)(2,1)} async-done(((bf16[384,768]{1,0:T(8,128)(2,1)}), bf16[384,1536]{1,0:T(8,128)(2,1)}) %all-gather.5.cloned.1.call-update) | async-done | bytes 1179664 | tf_op jit(solution)/shard_map/all_gather | solution.py:29
  69.6 17.0 %fusion.2 = (bf16[384,3072]{1,0:T(8,128)(2,1)S(1)}, f32[384,3072]{1,0:T(8,128)}) fusion(f32[3072]{0:T(1024)S(1)} %copy-done.10, bf16[384,1536]{1,0:T(8,128)(2,1)} %all-gather.5.cloned.1.call-done, bf16[1536,3072]{1,0:T(8,128)(2,1)} %param.16), kind=kOutput, calls=%fused_computation.53 | convolution fusion | flops 3701735424 | bytes 17707008 | tf_op jit(solution)/shard_map/dot_general | solution.py:109
  86.6 1.4 copy-done.3
  88.0 7.7 fusion.176
  95.7 0.0 reduce-scatter.5.cloned.1.call-update
  95.7 0.0 all-gather.7.cloned.1.call-start
  95.8 34.9 %reduce-scatter.5.cloned.1.call-done = f32[384,768]{1,0:T(8,128)} async-done(((f32[384,1536]{1,0:T(8,128)}), f32[384,768]{1,0:T(8,128)}) %reduce-scatter.5.cloned.1.call-update) | async-done | bytes 1179664 | tf_op jit(solution)/shard_map/reduce_scatter | solution.py:37
  130.7 2.9 fusion.158
  133.6 0.2 reduce-scatter.9.cloned.1.call-start
  133.8 22.7 %all-gather.7.cloned.1.call-done = bf16[384,1536]{1,0:T(8,128)(2,1)} async-done(((bf16[384,768]{1,0:T(8,128)(2,1)}), bf16[384,1536]{1,0:T(8,128)(2,1)}) %all-gather.7.cloned.1.call-update) | async-done | bytes 1179664 | tf_op jit(solution)/shard_map/all_gather | solution.py:29
  156.5 8.4 fusion.8
  164.9 1.4 copy-done.4
  166.3 9.5 %fusion.178 = f32[1536,3072]{1,0:T(8,128)} fusion(bf16[384,1536]{1,0:T(8,128)(2,1)S(1)} %copy-done.6, bf16[384,3072]{1,0:T(8,128)(2,1)S(1)} %fusion.8), kind=kOutput, calls=%fused_computation.401 | convolution fusion | flops 3623878656 | bytes 22413312 | tf_op jit(solution)/shard_map/dot_general | solution.py:133
  175.8 0.0 reduce-scatter.11.cloned.1.call-start
  175.9 14.2 %fusion.179 = f32[3072,1536]{0,1:T(8,128)} fusion(bf16[384,3072]{1,0:T(8,128)(2,1)} %copy-done.3, bf16[384,1536]{1,0:T(8,128)(2,1)} %all-gather.7.cloned.1.call-done), kind=kOutput, calls=%fused_computation.402 | convolution fusion | flops 3623878656 | bytes 22413312 | tf_op jit(solution)/shard_map/dot_general | solution.py:123
  190.1 0.0 reduce-scatter.7.cloned.1.call-start
  190.1 12.0 %fusion.177 = f32[384,1536]{1,0:T(8,128)} fusion(bf16[384,3072]{1,0:T(8,128)(2,1)} %copy-done.4, bf16[1536,3072]{1,0:T(8,128)(2,1)} %param.16), kind=kOutput, calls=%fused_computation.400 | convolution fusion | flops 3623878656 | bytes 14155776 | tf_op jit(solution)/shard_map/dot_general | solution.py:138
  202.2 0.0 all-gather.9.cloned.1.call-start
  202.2 167.8 %reduce-scatter.9.cloned.1.call-done = f32[96,3072]{1,0:T(8,128)} async-done(((f32[1536,3072]{1,0:T(8,128)}), f32[96,3072]{1,0:T(8,128)}) %reduce-scatter.9.cloned.1.call-update) | async-done | bytes 1179664 | tf_op jit(solution)/shard_map/reduce_scatter | solution.py:41
  370.0 2.2 convert_element_type.100
  372.2 0.0 all-gather.11.cloned.1.call-start
  372.2 195.5 %reduce-scatter.11.cloned.1.call-done = f32[3072,96]{0,1:T(8,128)} async-done(((f32[3072,1536]{0,1:T(8,128)}), f32[3072,96]{0,1:T(8,128)}) %reduce-scatter.11.cloned.1.call-update) | async-done | bytes 1179664 | tf_op jit(solution)/shard_map/reduce_scatter | solution.py:41
  567.7 2.2 convert_element_type.102
  569.9 0.0 all-reduce.4.cloned.1.call-start
  569.9 33.8 %reduce-scatter.7.cloned.1.call-done = f32[384,768]{1,0:T(8,128)} async-done(((f32[384,1536]{1,0:T(8,128)}), f32[384,768]{1,0:T(8,128)}) %reduce-scatter.7.cloned.1.call-update) | async-done | bytes 1179664 | tf_op jit(solution)/shard_map/reduce_scatter | solution.py:37
  603.7 1.7 multiply_reduce_fusion.2
  605.4 5.2 psum.30
  610.6 1.6 multiply_convert_fusion
  612.3 2.0 fusion.153
  614.5 2.9 fusion.154
  617.4 2.9 fusion.155
  620.8 3.5 collective-permute-start.2
  624.3 1.3 collective-permute-start.3
  626.1 0.7 copy-done.7
  626.8 7.3 collective-permute-done.2
  634.1 7.4 collective-permute-done.3
  641.5 0.2 maximum_convert_fusion.1
  641.6 9.7 %fusion.104 = bf16[1,8,48,768]{3,2,1,0:T(8,128)(2,1)} fusion(f32[1,14,48,768]{3,2,1,0:T(8,128)S(1)} %maximum_convert_fusion.1, f32[768]{0:T(1024)S(1)} %get-tuple-element.109, f32[768]{0:T(1024)S(1)} %get-tuple-element.62, f32[768]{0:T(1024)S(1)} %get-tuple-element.63, f32[768]{0:T(1024)S(1)} %get-tuple-element.64, f32[768]{0:T(1024)S(1)} %get-tuple-element.65, ...), kind=kLoop, calls=%fused_computation.247 | loop fusion | flops 29491200 | bytes 11702272 | tf_op jit(solution)/shard_map/convert_element_type | solution.py:159
  651.3 41.1 %all-gather.9.cloned.1.call-done = bf16[1536,3072]{1,0:T(8,128)(2,1)} async-done(((bf16[96,3072]{1,0:T(8,128)(2,1)}), bf16[1536,3072]{1,0:T(8,128)(2,1)}) %all-gather.9.cloned.1.call-update) | async-done | bytes 9437200 | tf_op jit(solution)/shard_map/all_gather | solution.py:42
  692.4 12.7 %convert_element_type.101 = f32[1536,3072]{1,0:T(8,128)} convert(bf16[1536,3072]{1,0:T(8,128)(2,1)} %all-gather.9.cloned.1.call-done) | non-fusion elementwise | flops 4718592 | bytes 28311552 | tf_op jit(solution)/shard_map/convert_element_type | solution.py:43
  705.1 68.9 %all-gather.11.cloned.1.call-done = bf16[3072,1536]{0,1:T(8,128)(2,1)} async-done(((bf16[3072,96]{0,1:T(8,128)(2,1)}), bf16[3072,1536]{0,1:T(8,128)(2,1)}) %all-gather.11.cloned.1.call-update) | async-done | bytes 9437200 | tf_op jit(solution)/shard_map/all_gather | solution.py:42
  774.0 13.5 %copy.16 = f32[3072,1536]{1,0:T(8,128)} copy(bf16[3072,1536]{0,1:T(8,128)(2,1)} %all-gather.11.cloned.1.call-done) | data formatting | bytes 28311552
  787.5 78.1 %all-reduce.4.cloned.1.call-done = f32[7,7,768]{2,1,0:T(8,128)} async-done(((f32[7,7,768]{2,1,0:T(8,128)}), f32[7,7,768]{2,1,0:T(8,128)}) %all-reduce.4.cloned.1.call-update) | async-done | bytes 150544 | tf_op jit(solution)/shard_map/psum | solution.py:160
  865.6 1.6 copy.24
  (98 shorter events, 0.8 us)
Async XLA Ops:
  7.2 14.9 %copy-start.2 = (bf16[1,8,48,768]{3,2,1,0:T(8,128)(2,1)S(1)}, bf16[1,8,48,768]{3,2,1,0:T(8,128)(2,1)}, u32[]{:S(2)}) copy-start(bf16[1,8,48,768]{3,2,1,0:T(8,128)(2,1)} %param.11) | copy-start | bytes 1769476
  7.2 62.4 %all-gather.5.cloned.1.call-start = ((), (), s32[]{:S(2)}) async-start(), calls=%async_computation.4 | async-start | bytes 1769472 | tf_op jit(solution)/shard_map/all_gather | solution.py:29
  8.4 11.0 %collective-permute-start = (bf16[1,3,48,768]{3,2,1,0:T(8,128)(2,1)S(1)}, bf16[1,3,48,768]{3,2,1,0:T(8,128)(2,1)S(1)}, u32[]{:S(2)}, u32[]{:S(2)}) collective-permute-start(bf16[1,3,48,768]{3,2,1,0:T(8,128)(2,1)S(1)} %get-tuple-element.116), channel_id=1, source_target_pairs={{0,2},{2,4},{4,6},{1,3},{3,5},{5,7},{8,10},{10,12},{12,14},{9,11},... | collective-permute-start | bytes 663560 | tf_op jit(solution)/shard_map/ppermute | solution.py:16
  13.3 8.8 %collective-permute-start.1 = (bf16[1,3,48,768]{3,2,1,0:T(8,128)(2,1)S(1)}, bf16[1,3,48,768]{3,2,1,0:T(8,128)(2,1)S(1)}, u32[]{:S(2)}, u32[]{:S(2)}) collective-permute-start(bf16[1,3,48,768]{3,2,1,0:T(8,128)(2,1)S(1)} %get-tuple-element.117), channel_id=1, source_target_pairs={{2,0},{4,2},{6,4},{3,1},{5,3},{7,5},{10,8},{12,10},{14,12},{11,9},... | collective-permute-start | bytes 663560 | tf_op jit(solution)/shard_map/ppermute | solution.py:19
  45.4 24.2 %copy-start.10 = (f32[3072]{0:T(1024)S(1)}, f32[3072]{0:T(1024)}, u32[]{:S(2)}) copy-start(f32[3072]{0:T(1024)} %param.17) | copy-start | bytes 36868
  46.5 84.2 %reduce-scatter.5.cloned.1.call-start = ((), (), s32[]{:S(2)}) async-start(), calls=%async_computation.5 | async-start | bytes 3538944 | tf_op jit(solution)/shard_map/reduce_scatter | solution.py:37
  86.6 1.4 copy-start.3
  95.7 35.0 %copy-start.8 = (f32[768]{0:T(1024)S(1)}, f32[768]{0:T(1024)}, u32[]{:S(2)}) copy-start(f32[768]{0:T(1024)} %param.20) | copy-start | bytes 9220
  95.7 35.0 %copy-start.9 = (f32[768]{0:T(1024)S(1)}, f32[768]{0:T(1024)}, u32[]{:S(2)}) copy-start(f32[768]{0:T(1024)} %param.19) | copy-start | bytes 9220
  95.7 60.7 %all-gather.7.cloned.1.call-start = ((), (), s32[]{:S(2)}) async-start(), calls=%async_computation.6 | async-start | bytes 1769472 | tf_op jit(solution)/shard_map/all_gather | solution.py:29
  133.6 236.4 %reduce-scatter.9.cloned.1.call-start = ((), (), s32[]{:S(2)}) async-start(), calls=%async_computation.8 | async-start | bytes 20054016 | tf_op jit(solution)/shard_map/reduce_scatter | solution.py:41
  156.5 9.8 %copy-start.6 = (bf16[384,1536]{1,0:T(8,128)(2,1)S(1)}, bf16[384,1536]{1,0:T(8,128)(2,1)}, u32[]{:S(2)}) copy-start(bf16[384,1536]{1,0:T(8,128)(2,1)} %all-gather.5.cloned.1.call-done) | copy-start | bytes 3538948
  164.9 1.4 copy-start.4
  175.8 391.9 %reduce-scatter.11.cloned.1.call-start = ((), (), s32[]{:S(2)}) async-start(), calls=%async_computation.10 | async-start | bytes 20054016 | tf_op jit(solution)/shard_map/reduce_scatter | solution.py:41
  190.1 413.7 %reduce-scatter.7.cloned.1.call-start = ((), (), s32[]{:S(2)}) async-start(), calls=%async_computation.7 | async-start | bytes 3538944 | tf_op jit(solution)/shard_map/reduce_scatter | solution.py:37
  202.2 490.2 %all-gather.9.cloned.1.call-start = ((), (), s32[]{:S(2)}) async-start(), calls=%async_computation.9 | async-start | bytes 10027008 | tf_op jit(solution)/shard_map/all_gather | solution.py:42
  372.2 401.8 %all-gather.11.cloned.1.call-start = ((), (), s32[]{:S(2)}) async-start(), calls=%async_computation.11 | async-start | bytes 10027008 | tf_op jit(solution)/shard_map/all_gather | solution.py:42
  569.9 295.7 %all-reduce.4.cloned.1.call-start = ((), (), s32[]{:S(2)}) async-start(), calls=%async_computation.12 | async-start | bytes 344064 | tf_op jit(solution)/shard_map/psum | solution.py:160
  612.2 8.5 copy-start
  620.8 20.7 %copy-start.1 = (bf16[384,768]{1,0:T(8,128)(2,1)S(1)}, bf16[384,768]{1,0:T(8,128)(2,1)}, u32[]{:S(2)}) copy-start(bf16[384,768]{1,0:T(8,128)(2,1)} %copy-done) | copy-start | bytes 1769476
  620.8 13.3 %collective-permute-start.2 = (bf16[1,3,48,768]{3,2,1,0:T(8,128)(2,1)S(1)}, bf16[1,3,48,768]{3,2,1,0:T(8,128)(2,1)S(1)}, u32[]{:S(2)}, u32[]{:S(2)}) collective-permute-start(bf16[1,3,48,768]{3,2,1,0:T(8,128)(2,1)S(1)} %get-tuple-element.114), channel_id=1, source_target_pairs={{0,2},{2,4},{4,6},{1,3},{3,5},{5,7},{8,10},{10,12},{12,14},{9,11},... | collective-permute-start | bytes 663560 | tf_op jit(solution)/shard_map/ppermute | solution.py:16
  624.3 17.1 %collective-permute-start.3 = (bf16[1,3,48,768]{3,2,1,0:T(8,128)(2,1)S(1)}, bf16[1,3,48,768]{3,2,1,0:T(8,128)(2,1)S(1)}, u32[]{:S(2)}, u32[]{:S(2)}) collective-permute-start(bf16[1,3,48,768]{3,2,1,0:T(8,128)(2,1)S(1)} %get-tuple-element.115), channel_id=1, source_target_pairs={{2,0},{4,2},{6,4},{3,1},{5,3},{7,5},{10,8},{12,10},{14,12},{11,9},... | collective-permute-start | bytes 663560 | tf_op jit(solution)/shard_map/ppermute | solution.py:19
  626.1 0.7 copy-start.7
  626.8 14.9 %copy-start.5 = (bf16[1,8,48,768]{3,2,1,0:T(8,128)(2,1)S(1)}, bf16[1,8,48,768]{3,2,1,0:T(8,128)(2,1)}, u32[]{:S(2)}) copy-start(bf16[1,8,48,768]{3,2,1,0:T(8,128)(2,1)} %param.21) | copy-start | bytes 1769476
Sparse Core Ops, SparseCore 0:
  46.6 22.9 all-gather.4
  95.8 34.7 reduce-scatter.4
  133.7 22.7 all-gather.6
  175.9 194.0 reduce-scatter.8
  374.5 193.1 reduce-scatter.10
  569.8 33.8 reduce-scatter.6
  606.6 85.7 all-gather.8
  694.7 79.2 all-gather.10
  778.0 87.5 all-reduce.3

commit v2 on v0

--- a/solution.py
+++ b/solution.py
@@ -35,6 +35,12 @@
 
 def partial_sums(term_rows):
     return lax.psum_scatter(term_rows, "tensor", scatter_dimension=1, tiled=True)
+
+
+def pixel_total(term, dim):
+    shared = lax.psum_scatter(term, ("dp", "space"), scatter_dimension=dim, tiled=True)
+    whole = lax.all_gather(shared.astype(jnp.bfloat16), ("dp", "space"), axis=dim, tiled=True)
+    return whole.astype(jnp.float32)
 
 
 def depthwise(padded, tap_weights, row_count, col_count):
@@ -113,20 +119,24 @@
         jnp.bfloat16
     )
     grad_full = all_channels(grad_scaled)
-    grad_project = lax.dot_general(
+    project_terms = lax.dot_general(
         activated, grad_full, (((0,), (0,)), ((), ())), preferred_element_type=jnp.float32
     )
     grad_act = lax.dot_general(
         grad_full, project_weight, (((1,), (1,)), ((), ())), preferred_element_type=jnp.float32
     )
     grad_hidden = (grad_act * gelu_slope(hidden)).astype(jnp.bfloat16)
-    grad_expand = lax.dot_general(
+    expand_terms = lax.dot_general(
         gathered, grad_hidden, (((0,), (0,)), ((), ())), preferred_element_type=jnp.float32
     )
     normed_terms = lax.dot_general(
         grad_hidden, expand_weight, (((1,), (1,)), ((), ())), preferred_element_type=jnp.float32
     )
     grad_normed = partial_sums(normed_terms)
+    grad_normed, project_terms, expand_terms = lax.optimization_barrier(
+        (grad_normed, project_terms, expand_terms)
+    )
+    grad_project = pixel_total(project_terms, 1)
     scaled_grad = grad_normed * own_gain
     channel_means = (
         lax.psum(
@@ -145,9 +155,16 @@
         cotangent.astype(jnp.float32)
         + depthwise(grad_padded, own_kernel[::-1, ::-1], row_count, col_count)
     ).astype(jnp.bfloat16)
-    grad_expand, grad_project, grad_kernel = lax.psum(
-        (grad_expand, grad_project, grad_kernel), ("dp", "space")
+    kernel_flat = grad_kernel.reshape(-1)
+    hidden_shard = expand_terms.shape[1]
+    extra = -(-kernel_flat.size // hidden_shard)
+    extra = -(-(full_width + extra) // 8) * 8 - full_width
+    kernel_rows = jnp.pad(kernel_flat, (0, extra * hidden_shard - kernel_flat.size)).reshape(
+        extra, hidden_shard
     )
+    merged = pixel_total(jnp.concatenate([expand_terms, kernel_rows]), 1)
+    grad_expand = merged[:full_width]
+    grad_kernel = merged[full_width:].reshape(-1)[: kernel_flat.size].reshape(grad_kernel.shape)
     return (block_out, grad_input, grad_expand, grad_project, grad_kernel)
 
 

time: 899 us -> 845 us (0.940)
  waiting for transfers between devices: 721 us -> 585 us
  local copies, waits for them, and re-layouts: 36.8 us -> 95.9 us
  other arithmetic: 38.1 us -> 60.2 us
    psum x1 -> x0, waiting for transfers between devices: 611 us -> none  [body(): lax.psum((grad_expand, grad_project, grad_kernel), ('dp', 'space'))]
    unnamed x5 -> x10, waiting for transfers between devices: 0.08 us -> 347 us
    all_gather x0 -> x2, waiting for transfers between devices: none -> 133 us  [pixel_total(): lax.all_gather(shared.astype(jnp.bfloat16), ('dp', 'space'), axis=dim, ti...]
    unnamed x37 -> x33, local copies, waits for them, and re-layouts: 30.1 us -> 73.9 us
    concatenate x0 -> x1, other arithmetic: none -> 17.8 us  [body(): merged = pixel_total(jnp.concatenate([expand_terms, kernel_rows]), 1)]
    slice x0 -> x4, local copies, waits for them, and re-layouts: none -> 14.5 us  [the longest x1 12.8 us: body(): grad_expand = merged[:full_width]]
  transfers between devices with their start and end apart: 9 -> 12, of which waited for: 8 -> 11; matrix products, arithmetic and copies ran while one was open for 4% -> 12% of each run, Pallas kernels for 0% -> 0%
where the time goes in v2:
time: 845 us; the launch traced here: 843 us
  waiting for transfers between devices  585 us (69%)
  local copies, waits for them, and re-layouts  95.9 us (11%)
  matrix products  61.6 us (7%)
  other arithmetic  60.2 us (7%)
  blocking collectives  15 us (2%)
  between operations  14.9 us (2%)
  starting transfers between devices  10.3 us (1%)
    unnamed x10, waiting for transfers between devices  347 us
    all_gather x2, waiting for transfers between devices, pixel_total(): lax.all_gather(shared.astype(jnp.bfloat16), ('dp', 'space'), axis=dim, ti...  133 us
    unnamed x33, local copies, waits for them, and re-layouts  73.9 us
    reduce_scatter x2, waiting for transfers between devices, partial_sums(): lax.psum_scatter(term_rows, 'tensor', scatter_dimension=1, tiled=True)  49 us
    all_gather x2, waiting for transfers between devices, all_channels(): return lax.all_gather(block_data, 'tensor', axis=1, tiled=True)  45.8 us
    concatenate x1, other arithmetic, body(): merged = pixel_total(jnp.concatenate([expand_terms, kernel_rows]), 1)  17.8 us
    dot_general x1, matrix products, body(): jnp.dot(gathered, expand_weight, preferred_element_type=jnp.float32)  17 us
  transfers between devices with their start and end apart: 12, of which 11 were waited for; matrix products, arithmetic and copies ran while one was open for 12% of the time, Pallas kernels for 0%

profile of v2, /device:TPU:0, one launch (start us, length us, event | category | flops | bytes accessed | tf_op | source)
XLA Modules:
  0.0 843.1 jit_solution(13579261890207634058)
XLA Ops:
  7.2 1.1 fusion.175
  8.4 5.0 collective-permute-start
  13.3 1.3 collective-permute-start.1
  14.6 0.8 dynamic_slice.14
  15.4 0.8 dynamic_slice.13
  16.2 0.8 dynamic_slice.15
  17.0 2.4 fusion.161
  19.4 2.7 collective-permute-done.1
  22.1 0.2 maximum_convert_fusion
  22.3 12.7 %fusion.173 = (f32[8,48]{1,0:T(8,128)S(1)}, f32[1,8,48,768]{3,2,1,0:T(8,128)S(1)}) fusion(f32[768]{0:T(1024)S(1)} %dynamic_slice.13, f32[768]{0:T(1024)S(1)} %get-tuple-element.125, f32[768]{0:T(1024)S(1)} %get-tuple-element.78, f32[768]{0:T(1024)S(1)} %get-tuple-element.79, f32[1,14,48,768]{3,2,1,0:T(8,128)S(1)} %maximum_convert_fusion, ...), kind=kLoop, calls=%fused_computation.399 | loop fusion | flops 29195904 | bytes 11707904 | tf_op jit(solution)/shard_map/reduce_sum | solution.py:103
  35.0 0.1 reduce_sum.482
  35.1 4.9 psum.21
  40.0 0.1 sub.30
  40.1 0.3 multiply_reduce_fusion.1
  40.4 0.1 reduce_sum.484
  40.4 4.9 psum.22
  45.4 1.1 add_convert_fusion
  46.5 0.0 reduce-scatter.9.cloned.1.call-start
  46.5 23.1 %all-gather.5.cloned.1.call-done = bf16[384,1536]{1,0:T(8,128)(2,1)} async-done(((bf16[384,768]{1,0:T(8,128)(2,1)}), bf16[384,1536]{1,0:T(8,128)(2,1)}) %all-gather.5.cloned.1.call-update) | async-done | bytes 1179664 | tf_op jit(solution)/shard_map/all_gather | solution.py:29
  69.6 17.0 %fusion.2 = (bf16[384,3072]{1,0:T(8,128)(2,1)S(1)}, f32[384,3072]{1,0:T(8,128)}) fusion(f32[3072]{0:T(1024)S(1)} %copy-done.10, bf16[384,1536]{1,0:T(8,128)(2,1)} %all-gather.5.cloned.1.call-done, bf16[1536,3072]{1,0:T(8,128)(2,1)} %param.16), kind=kOutput, calls=%fused_computation.54 | convolution fusion | flops 3701735424 | bytes 17707008 | tf_op jit(solution)/shard_map/dot_general | solution.py:109
  86.6 1.4 copy-done.3
  88.0 7.7 fusion.176
  95.7 0.0 all-gather.7.cloned.1.call-start
  95.8 34.9 %reduce-scatter.9.cloned.1.call-done = f32[384,768]{1,0:T(8,128)} async-done(((f32[384,1536]{1,0:T(8,128)}), f32[384,768]{1,0:T(8,128)}) %reduce-scatter.9.cloned.1.call-update) | async-done | bytes 1179664 | tf_op jit(solution)/shard_map/reduce_scatter | solution.py:37
  130.7 2.9 fusion.158
  133.6 0.2 reduce-scatter.11.cloned.1.call-start
  133.8 22.7 %all-gather.7.cloned.1.call-done = bf16[384,1536]{1,0:T(8,128)(2,1)} async-done(((bf16[384,768]{1,0:T(8,128)(2,1)}), bf16[384,1536]{1,0:T(8,128)(2,1)}) %all-gather.7.cloned.1.call-update) | async-done | bytes 1179664 | tf_op jit(solution)/shard_map/all_gather | solution.py:29
  156.5 8.3 fusion.8
  164.8 1.4 copy-done.5
  166.2 7.8 fusion.177
  174.0 0.0 reduce-scatter.15.cloned.1.call-start
  174.1 11.3 %fusion.179 = f32[1536,3072]{1,0:T(8,128)} fusion(bf16[384,1536]{1,0:T(8,128)(2,1)} %all-gather.5.cloned.1.call-done, bf16[384,3072]{1,0:T(8,128)(2,1)} %copy-done.5), kind=kOutput, calls=%fused_computation.405 | convolution fusion | flops 3623878656 | bytes 22413312 | tf_op jit(solution)/shard_map/dot_general | solution.py:129
  185.4 9.5 %fusion.178 = f32[3072,1536]{1,0:T(8,128)} fusion(bf16[384,3072]{1,0:T(8,128)(2,1)S(1)} %copy-done.4, bf16[384,1536]{1,0:T(8,128)(2,1)S(1)} %copy-done.7), kind=kOutput, calls=%fused_computation.404 | convolution fusion | flops 3623878656 | bytes 22413312 | tf_op jit(solution)/shard_map/dot_general | solution.py:122
  194.9 14.1 %reduce-scatter.11.cloned.1.call-done = f32[384,768]{1,0:T(8,128)} async-done(((f32[384,1536]{1,0:T(8,128)}), f32[384,768]{1,0:T(8,128)}) %reduce-scatter.11.cloned.1.call-update) | async-done | bytes 1179664 | tf_op jit(solution)/shard_map/reduce_scatter | solution.py:37
  209.0 18.6 %copy.32 = f32[3072,1536]{0,1:T(8,128)} copy(f32[3072,1536]{1,0:T(8,128)} %fusion.178) | data formatting | bytes 37748736
  227.6 0.0 reduce-scatter.13.cloned.1.call-start
  227.6 1.7 multiply_reduce_fusion.2
  229.3 5.2 psum.23
  234.5 1.6 multiply_convert_fusion
  236.2 2.0 fusion.153
  238.4 2.9 fusion.154
  241.3 2.9 fusion.155
  245.2 17.8 %pad_maximum_fusion = f32[1552,3072]{1,0:T(8,128)} fusion(f32[16,3072]{1,0:T(8,128)S(1)} %reshape.451, f32[1536,3072]{1,0:T(8,128)} %fusion.179), kind=kLoop, calls=%fused_computation | loop fusion | flops 4767744 | bytes 38141952 | tf_op jit(solution)/shard_map/concatenate | solution.py:165
  263.0 20.1 %copy.30 = f32[1552,3072]{0,1:T(8,128)} copy(f32[1552,3072]{1,0:T(8,128)} %pad_maximum_fusion) | data formatting | bytes 38141952
  283.1 0.0 all-gather.11.cloned.1.call-start
  283.1 138.7 %reduce-scatter.15.cloned.1.call-done = f32[96,3072]{1,0:T(8,128)} async-done(((f32[1536,3072]{1,0:T(8,128)}), f32[96,3072]{1,0:T(8,128)}) %reduce-scatter.15.cloned.1.call-update) | async-done | bytes 1179664
  421.8 2.2 bitcast_convert_fusion.1
  424.0 0.0 all-gather.9.cloned.1.call-start
  424.1 208.2 %reduce-scatter.13.cloned.1.call-done = f32[192,1552]{1,0:T(8,128)} async-done(((f32[3072,1552]{1,0:T(8,128)}), f32[192,1552]{1,0:T(8,128)}) %reduce-scatter.13.cloned.1.call-update) | async-done | bytes 1191952
  632.3 2.2 bitcast_convert_fusion
  634.6 2.1 collective-permute-start.2
  636.7 1.4 collective-permute-start.3
  638.1 2.8 collective-permute-done.2
  640.9 5.3 collective-permute-done.3
  646.2 0.2 maximum_convert_fusion.1
  646.4 9.7 %fusion.104 = bf16[1,8,48,768]{3,2,1,0:T(8,128)(2,1)} fusion(f32[1,14,48,768]{3,2,1,0:T(8,128)S(1)} %maximum_convert_fusion.1, f32[768]{0:T(1024)S(1)} %get-tuple-element.125, f32[768]{0:T(1024)S(1)} %get-tuple-element.78, f32[768]{0:T(1024)S(1)} %get-tuple-element.79, f32[768]{0:T(1024)S(1)} %get-tuple-element.80, f32[768]{0:T(1024)S(1)} %get-tuple-element.81, ...), kind=kLoop, calls=%fused_computation.249 | loop fusion | flops 29491200 | bytes 11702272 | tf_op jit(solution)/shard_map/convert_element_type | solution.py:157
  656.1 59.1 %all-gather.11.cloned.1.call-done = bf16[3072,1536]{0,1:T(8,128)(2,1)} async-done(((bf16[3072,96]{0,1:T(8,128)(2,1)}), bf16[3072,1536]{0,1:T(8,128)(2,1)}) %all-gather.11.cloned.1.call-update) | async-done | bytes 9437200 | tf_op jit(solution)/shard_map/all_gather | solution.py:42
  715.2 13.6 %copy.29 = f32[3072,1536]{1,0:T(8,128)} copy(bf16[3072,1536]{0,1:T(8,128)(2,1)} %all-gather.11.cloned.1.call-done) | data formatting | bytes 28311552
  728.8 73.6 %all-gather.9.cloned.1.call-done = bf16[1552,3072]{0,1:T(8,128)(2,1)} async-done(((bf16[1552,192]{0,1:T(8,128)(2,1)}), bf16[1552,3072]{0,1:T(8,128)(2,1)}) %all-gather.9.cloned.1.call-update) | async-done | bytes 9535504 | tf_op jit(solution)/shard_map/all_gather | solution.py:42
  802.4 1.2 slice.804
  803.6 0.4 copy.27
  804.1 0.7 reshape.453
  804.8 12.8 %slice.803 = f32[1536,3072]{0,1:T(8,128)} slice(bf16[1552,3072]{0,1:T(8,128)(2,1)} %all-gather.9.cloned.1.call-done), slice={[0:1536], [0:3072]} | slice | bytes 37748736 | tf_op jit(solution)/shard_map/slice | solution.py:166
  817.7 18.6 %copy.28 = f32[1536,3072]{1,0:T(8,128)} copy(f32[1536,3072]{0,1:T(8,128)} %slice.803) | data formatting | bytes 37748736
  (106 shorter events, 1.0 us)
Async XLA Ops:
  7.2 14.9 %copy-start.2 = (bf16[1,8,48,768]{3,2,1,0:T(8,128)(2,1)S(1)}, bf16[1,8,48,768]{3,2,1,0:T(8,128)(2,1)}, u32[]{:S(2)}) copy-start(bf16[1,8,48,768]{3,2,1,0:T(8,128)(2,1)} %param.11) | copy-start | bytes 1769476
  7.2 62.4 %all-gather.5.cloned.1.call-start = ((), (), s32[]{:S(2)}) async-start(), calls=%async_computation.4 | async-start | bytes 1769472 | tf_op jit(solution)/shard_map/all_gather | solution.py:29
  8.4 11.0 %collective-permute-start = (bf16[1,3,48,768]{3,2,1,0:T(8,128)(2,1)S(1)}, bf16[1,3,48,768]{3,2,1,0:T(8,128)(2,1)S(1)}, u32[]{:S(2)}, u32[]{:S(2)}) collective-permute-start(bf16[1,3,48,768]{3,2,1,0:T(8,128)(2,1)S(1)} %get-tuple-element.132), channel_id=1, source_target_pairs={{0,2},{2,4},{4,6},{1,3},{3,5},{5,7},{8,10},{10,12},{12,14},{9,11},... | collective-permute-start | bytes 663560 | tf_op jit(solution)/shard_map/ppermute | solution.py:16
  13.3 8.8 %collective-permute-start.1 = (bf16[1,3,48,768]{3,2,1,0:T(8,128)(2,1)S(1)}, bf16[1,3,48,768]{3,2,1,0:T(8,128)(2,1)S(1)}, u32[]{:S(2)}, u32[]{:S(2)}) collective-permute-start(bf16[1,3,48,768]{3,2,1,0:T(8,128)(2,1)S(1)} %get-tuple-element.133), channel_id=1, source_target_pairs={{2,0},{4,2},{6,4},{3,1},{5,3},{7,5},{10,8},{12,10},{14,12},{11,9},... | collective-permute-start | bytes 663560 | tf_op jit(solution)/shard_map/ppermute | solution.py:19
  45.4 24.2 %copy-start.10 = (f32[3072]{0:T(1024)S(1)}, f32[3072]{0:T(1024)}, u32[]{:S(2)}) copy-start(f32[3072]{0:T(1024)} %param.17) | copy-start | bytes 36868
  46.5 84.2 %reduce-scatter.9.cloned.1.call-start = ((), (), s32[]{:S(2)}) async-start(), calls=%async_computation.5 | async-start | bytes 3538944 | tf_op jit(solution)/shard_map/reduce_scatter | solution.py:37
  86.6 1.4 copy-start.3
  95.7 35.0 %copy-start.8 = (f32[768]{0:T(1024)S(1)}, f32[768]{0:T(1024)}, u32[]{:S(2)}) copy-start(f32[768]{0:T(1024)} %param.20) | copy-start | bytes 9220
  95.7 35.0 %copy-start.9 = (f32[768]{0:T(1024)S(1)}, f32[768]{0:T(1024)}, u32[]{:S(2)}) copy-start(f32[768]{0:T(1024)} %param.19) | copy-start | bytes 9220
  95.7 60.8 %all-gather.7.cloned.1.call-start = ((), (), s32[]{:S(2)}) async-start(), calls=%async_computation.6 | async-start | bytes 1769472 | tf_op jit(solution)/shard_map/all_gather | solution.py:29
  133.6 75.4 %reduce-scatter.11.cloned.1.call-start = ((), (), s32[]{:S(2)}) async-start(), calls=%async_computation.7 | async-start | bytes 3538944 | tf_op jit(solution)/shard_map/reduce_scatter | solution.py:37
  164.8 1.4 copy-start.5
  174.0 247.8 %reduce-scatter.15.cloned.1.call-start = ((), (), s32[]{:S(2)}) async-start(), calls=%async_computation.11 | async-start | bytes 20054016
  174.1 11.3 %copy-start.4 = (bf16[384,3072]{1,0:T(8,128)(2,1)S(1)}, bf16[384,3072]{1,0:T(8,128)(2,1)}, u32[]{:S(2)}) copy-start(bf16[384,3072]{1,0:T(8,128)(2,1)} %copy-done.3) | copy-start | bytes 7077892
  174.1 11.3 %copy-start.7 = (bf16[384,1536]{1,0:T(8,128)(2,1)S(1)}, bf16[384,1536]{1,0:T(8,128)(2,1)}, u32[]{:S(2)}) copy-start(bf16[384,1536]{1,0:T(8,128)(2,1)} %all-gather.7.cloned.1.call-done) | copy-start | bytes 3538948
  227.6 404.7 %reduce-scatter.13.cloned.1.call-start = ((), (), s32[]{:S(2)}) async-start(), calls=%async_computation.10 | async-start | bytes 21725184
  236.2 5.2 copy-start
  283.1 432.1 %all-gather.11.cloned.1.call-start = ((), (), s32[]{:S(2)}) async-start(), calls=%async_computation.9 | async-start | bytes 10027008 | tf_op jit(solution)/shard_map/all_gather | solution.py:42
  424.0 210.5 %copy-start.1 = (bf16[384,768]{1,0:T(8,128)(2,1)S(1)}, bf16[384,768]{1,0:T(8,128)(2,1)}, u32[]{:S(2)}) copy-start(bf16[384,768]{1,0:T(8,128)(2,1)} %copy-done) | copy-start | bytes 1769476
  424.0 378.4 %all-gather.9.cloned.1.call-start = ((), (), s32[]{:S(2)}) async-start(), calls=%async_computation.8 | async-start | bytes 10862592 | tf_op jit(solution)/shard_map/all_gather | solution.py:42
  634.6 6.3 collective-permute-start.2
  636.6 9.7 %copy-start.6 = (bf16[1,8,48,768]{3,2,1,0:T(8,128)(2,1)S(1)}, bf16[1,8,48,768]{3,2,1,0:T(8,128)(2,1)}, u32[]{:S(2)}) copy-start(bf16[1,8,48,768]{3,2,1,0:T(8,128)(2,1)} %param.21) | copy-start | bytes 1769476
  636.7 9.6 %collective-permute-start.3 = (bf16[1,3,48,768]{3,2,1,0:T(8,128)(2,1)S(1)}, bf16[1,3,48,768]{3,2,1,0:T(8,128)(2,1)S(1)}, u32[]{:S(2)}, u32[]{:S(2)}) collective-permute-start(bf16[1,3,48,768]{3,2,1,0:T(8,128)(2,1)S(1)} %get-tuple-element.131), channel_id=1, source_target_pairs={{2,0},{4,2},{6,4},{3,1},{5,3},{7,5},{10,8},{12,10},{14,12},{11,9},... | collective-permute-start | bytes 663560 | tf_op jit(solution)/shard_map/ppermute | solution.py:19
Sparse Core Ops, SparseCore 0:
  46.6 22.9 all-gather.4
  95.9 34.7 reduce-scatter.8
  133.7 22.7 all-gather.6
  174.1 34.7 reduce-scatter.10
  227.7 194.0 reduce-scatter.14
  425.9 206.3 reduce-scatter.12
  635.2 79.9 all-gather.10
  718.1 84.2 all-gather.8

commit v3 on v2

--- a/solution.py
+++ b/solution.py
@@ -136,7 +136,7 @@
     grad_normed, project_terms, expand_terms = lax.optimization_barrier(
         (grad_normed, project_terms, expand_terms)
     )
-    grad_project = pixel_total(project_terms, 1)
+    grad_project = pixel_total(project_terms, 0)
     scaled_grad = grad_normed * own_gain
     channel_means = (
         lax.psum(

time: 845 us -> 830 us (0.982)
  local copies, waits for them, and re-layouts: 95.9 us -> 63.1 us
  other arithmetic: 60.2 us -> 74.1 us
    reduce_scatter x0 -> x1, waiting for transfers between devices: none -> 143 us  [pixel_total(): lax.psum_scatter(term, ('dp', 'space'), scatter_dimension=dim, tiled=True)]
    unnamed x10 -> x9, waiting for transfers between devices: 347 us -> 208 us
    unnamed x33 -> x31, local copies, waits for them, and re-layouts: 73.9 us -> 41.3 us
    convert_element_type x0 -> x1, other arithmetic: none -> 13.3 us  [pixel_total(): return whole.astype(jnp.float32)]
where the time goes in v3:
time: 830 us; the launch traced here: 829 us
  waiting for transfers between devices  590 us (71%)
  other arithmetic  74.1 us (9%)
  local copies, waits for them, and re-layouts  63.1 us (8%)
  matrix products  61.6 us (7%)
  blocking collectives  15 us (2%)
  between operations  14.9 us (2%)
  starting transfers between devices  10.3 us (1%)
    unnamed x9, waiting for transfers between devices  208 us
    reduce_scatter x1, waiting for transfers between devices, pixel_total(): lax.psum_scatter(term, ('dp', 'space'), scatter_dimension=dim, tiled=True)  143 us
    all_gather x2, waiting for transfers between devices, pixel_total(): lax.all_gather(shared.astype(jnp.bfloat16), ('dp', 'space'), axis=dim, ti...  133 us
    reduce_scatter x2, waiting for transfers between devices, partial_sums(): lax.psum_scatter(term_rows, 'tensor', scatter_dimension=1, tiled=True)  48.9 us
    all_gather x2, waiting for transfers between devices, all_channels(): return lax.all_gather(block_data, 'tensor', axis=1, tiled=True)  45.8 us
    unnamed x31, local copies, waits for them, and re-layouts  41.3 us
    concatenate x1, other arithmetic, body(): merged = pixel_total(jnp.concatenate([expand_terms, kernel_rows]), 1)  18.3 us
    dot_general x1, matrix products, body(): jnp.dot(gathered, expand_weight, preferred_element_type=jnp.float32)  17 us
  transfers between devices with their start and end apart: 12, of which 11 were waited for; matrix products, arithmetic and copies ran while one was open for 12% of the time, Pallas kernels for 0%

profile of v3, /device:TPU:0, one launch (start us, length us, event | category | flops | bytes accessed | tf_op | source)
XLA Modules:
  0.0 828.9 jit_solution(12413500016732027997)
XLA Ops:
  7.2 0.0 all-gather.5.cloned.1.call-start
  7.2 1.1 fusion.175
  8.4 5.0 collective-permute-start
  13.3 1.3 collective-permute-start.1
  14.6 0.8 dynamic_slice.14
  15.4 0.8 dynamic_slice.13
  16.2 0.8 dynamic_slice.15
  17.0 2.2 fusion.161
  19.2 3.0 collective-permute-done.1
  22.1 0.2 maximum_convert_fusion
  22.3 12.7 %fusion.173 = (f32[8,48]{1,0:T(8,128)S(1)}, f32[1,8,48,768]{3,2,1,0:T(8,128)S(1)}) fusion(f32[768]{0:T(1024)S(1)} %dynamic_slice.13, f32[768]{0:T(1024)S(1)} %get-tuple-element.125, f32[768]{0:T(1024)S(1)} %get-tuple-element.78, f32[768]{0:T(1024)S(1)} %get-tuple-element.79, f32[1,14,48,768]{3,2,1,0:T(8,128)S(1)} %maximum_convert_fusion, ...), kind=kLoop, calls=%fused_computation.398 | loop fusion | flops 29195904 | bytes 11707904 | tf_op jit(solution)/shard_map/reduce_sum | solution.py:103
  35.0 0.1 reduce_sum.482
  35.1 4.9 psum.21
  40.0 0.1 sub.30
  40.1 0.3 multiply_reduce_fusion.1
  40.4 0.1 reduce_sum.484
  40.4 4.9 psum.22
  45.4 1.1 add_convert_fusion
  46.5 0.0 reduce-scatter.7.cloned.1.call-start
  46.5 23.1 %all-gather.5.cloned.1.call-done = bf16[384,1536]{1,0:T(8,128)(2,1)} async-done(((bf16[384,768]{1,0:T(8,128)(2,1)}), bf16[384,1536]{1,0:T(8,128)(2,1)}) %all-gather.5.cloned.1.call-update) | async-done | bytes 1179664 | tf_op jit(solution)/shard_map/all_gather | solution.py:29
  69.6 17.0 %fusion.2 = (bf16[384,3072]{1,0:T(8,128)(2,1)S(1)}, f32[384,3072]{1,0:T(8,128)}) fusion(f32[3072]{0:T(1024)S(1)} %copy-done.10, bf16[384,1536]{1,0:T(8,128)(2,1)} %all-gather.5.cloned.1.call-done, bf16[1536,3072]{1,0:T(8,128)(2,1)} %param.16), kind=kOutput, calls=%fused_computation.54 | convolution fusion | flops 3701735424 | bytes 17707008 | tf_op jit(solution)/shard_map/dot_general | solution.py:109
  86.6 1.4 copy-done.3
  88.0 7.7 fusion.176
  95.7 0.0 all-gather.7.cloned.1.call-start
  95.8 34.9 %reduce-scatter.7.cloned.1.call-done = f32[384,768]{1,0:T(8,128)} async-done(((f32[384,1536]{1,0:T(8,128)}), f32[384,768]{1,0:T(8,128)}) %reduce-scatter.7.cloned.1.call-update) | async-done | bytes 1179664 | tf_op jit(solution)/shard_map/reduce_scatter | solution.py:37
  130.7 2.9 fusion.158
  133.6 0.2 reduce-scatter.9.cloned.1.call-start
  133.8 22.7 %all-gather.7.cloned.1.call-done = bf16[384,1536]{1,0:T(8,128)(2,1)} async-done(((bf16[384,768]{1,0:T(8,128)(2,1)}), bf16[384,1536]{1,0:T(8,128)(2,1)}) %all-gather.7.cloned.1.call-update) | async-done | bytes 1179664 | tf_op jit(solution)/shard_map/all_gather | solution.py:29
  156.5 8.3 %fusion.8 = bf16[384,3072]{1,0:T(8,128)(2,1)S(1)} fusion(bf16[384,1536]{1,0:T(8,128)(2,1)} %all-gather.7.cloned.1.call-done, bf16[3072,1536]{1,0:T(8,128)(2,1)} %param.18, f32[384,3072]{1,0:T(8,128)} %get-tuple-element.137, f32[3072]{0:T(1024)S(1)} %copy-done.10), kind=kOutput, calls=%fused_computation.60 | convolution fusion | flops 3636854784 | bytes 17707008 | tf_op jit(solution)/shard_map/dot_general | solution.py:125
  164.8 1.4 copy-done.5
  166.2 7.8 fusion.177
  174.1 0.0 reduce-scatter.11.cloned.1.call-start
  174.1 11.3 %fusion.179 = f32[1536,3072]{1,0:T(8,128)} fusion(bf16[384,1536]{1,0:T(8,128)(2,1)} %all-gather.5.cloned.1.call-done, bf16[384,3072]{1,0:T(8,128)(2,1)} %copy-done.5), kind=kOutput, calls=%fused_computation.404 | convolution fusion | flops 3623878656 | bytes 22413312 | tf_op jit(solution)/shard_map/dot_general | solution.py:129
  185.4 9.5 %fusion.178 = f32[3072,1536]{1,0:T(8,128)} fusion(bf16[384,3072]{1,0:T(8,128)(2,1)S(1)} %copy-done.4, bf16[384,1536]{1,0:T(8,128)(2,1)S(1)} %copy-done.7), kind=kOutput, calls=%fused_computation.403 | convolution fusion | flops 3623878656 | bytes 22413312 | tf_op jit(solution)/shard_map/dot_general | solution.py:122
  194.9 14.0 %reduce-scatter.9.cloned.1.call-done = f32[384,768]{1,0:T(8,128)} async-done(((f32[384,1536]{1,0:T(8,128)}), f32[384,768]{1,0:T(8,128)}) %reduce-scatter.9.cloned.1.call-update) | async-done | bytes 1179664 | tf_op jit(solution)/shard_map/reduce_scatter | solution.py:37
  209.0 0.0 reduce-scatter.13.cloned.1.call-start
  209.1 1.7 multiply_reduce_fusion.2
  210.8 5.2 psum.23
  215.9 1.6 multiply_convert_fusion
  217.6 2.0 fusion.153
  219.8 2.9 fusion.154
  222.7 2.9 fusion.155
  226.6 18.3 %pad_maximum_fusion = f32[1552,3072]{1,0:T(8,128)} fusion(f32[16,3072]{1,0:T(8,128)S(1)} %reshape.451, f32[1536,3072]{1,0:T(8,128)} %fusion.179), kind=kLoop, calls=%fused_computation | loop fusion | flops 4767744 | bytes 38141952 | tf_op jit(solution)/shard_map/concatenate | solution.py:165
  244.9 19.7 %copy.24 = f32[1552,3072]{0,1:T(8,128)} copy(f32[1552,3072]{1,0:T(8,128)} %pad_maximum_fusion) | data formatting | bytes 38141952
  264.7 0.0 all-gather.11.cloned.1.call-start
  264.8 142.8 %reduce-scatter.11.cloned.1.call-done = f32[192,1536]{1,0:T(8,128)} async-done(((f32[3072,1536]{1,0:T(8,128)}), f32[192,1536]{1,0:T(8,128)}) %reduce-scatter.11.cloned.1.call-update) | async-done | bytes 1179664 | tf_op jit(solution)/shard_map/reduce_scatter | solution.py:41
  407.6 2.1 convert_element_type.105
  409.8 0.0 all-gather.9.cloned.1.call-start
  409.8 208.2 %reduce-scatter.13.cloned.1.call-done = f32[192,1552]{1,0:T(8,128)} async-done(((f32[3072,1552]{1,0:T(8,128)}), f32[192,1552]{1,0:T(8,128)}) %reduce-scatter.13.cloned.1.call-update) | async-done | bytes 1191952
  618.0 2.2 bitcast_convert_fusion
  620.3 2.1 collective-permute-start.2
  622.4 1.4 collective-permute-start.3
  623.8 2.8 collective-permute-done.2
  626.6 5.2 collective-permute-done.3
  631.9 0.2 maximum_convert_fusion.1
  632.1 9.7 %fusion.104 = bf16[1,8,48,768]{3,2,1,0:T(8,128)(2,1)} fusion(f32[1,14,48,768]{3,2,1,0:T(8,128)S(1)} %maximum_convert_fusion.1, f32[768]{0:T(1024)S(1)} %get-tuple-element.125, f32[768]{0:T(1024)S(1)} %get-tuple-element.78, f32[768]{0:T(1024)S(1)} %get-tuple-element.79, f32[768]{0:T(1024)S(1)} %get-tuple-element.80, f32[768]{0:T(1024)S(1)} %get-tuple-element.81, ...), kind=kLoop, calls=%fused_computation.249 | loop fusion | flops 29491200 | bytes 11702272 | tf_op jit(solution)/shard_map/convert_element_type | solution.py:157
  641.7 59.2 %all-gather.11.cloned.1.call-done = bf16[3072,1536]{1,0:T(8,128)(2,1)} async-done(((bf16[192,1536]{1,0:T(8,128)(2,1)}), bf16[3072,1536]{1,0:T(8,128)(2,1)}) %all-gather.11.cloned.1.call-update) | async-done | bytes 9437200 | tf_op jit(solution)/shard_map/all_gather | solution.py:42
  700.9 13.3 %convert_element_type.106 = f32[3072,1536]{1,0:T(8,128)} convert(bf16[3072,1536]{1,0:T(8,128)(2,1)} %all-gather.11.cloned.1.call-done) | non-fusion elementwise | flops 4718592 | bytes 28311552 | tf_op jit(solution)/shard_map/convert_element_type | solution.py:43
  714.2 73.9 %all-gather.9.cloned.1.call-done = bf16[1552,3072]{0,1:T(8,128)(2,1)} async-done(((bf16[1552,192]{0,1:T(8,128)(2,1)}), bf16[1552,3072]{0,1:T(8,128)(2,1)}) %all-gather.9.cloned.1.call-update) | async-done | bytes 9535504 | tf_op jit(solution)/shard_map/all_gather | solution.py:42
  788.1 1.2 slice.804
  789.4 0.4 copy.22
  789.9 0.7 reshape.453
  790.6 12.8 %slice.803 = f32[1536,3072]{0,1:T(8,128)} slice(bf16[1552,3072]{0,1:T(8,128)(2,1)} %all-gather.9.cloned.1.call-done), slice={[0:1536], [0:3072]} | slice | bytes 37748736 | tf_op jit(solution)/shard_map/slice | solution.py:166
  803.4 18.6 %copy.23 = f32[1536,3072]{1,0:T(8,128)} copy(f32[1536,3072]{0,1:T(8,128)} %slice.803) | data formatting | bytes 37748736
  (105 shorter events, 1.0 us)
Async XLA Ops:
  7.2 14.9 %copy-start.2 = (bf16[1,8,48,768]{3,2,1,0:T(8,128)(2,1)S(1)}, bf16[1,8,48,768]{3,2,1,0:T(8,128)(2,1)}, u32[]{:S(2)}) copy-start(bf16[1,8,48,768]{3,2,1,0:T(8,128)(2,1)} %param.11) | copy-start | bytes 1769476
  7.2 62.4 %all-gather.5.cloned.1.call-start = ((), (), s32[]{:S(2)}) async-start(), calls=%async_computation.4 | async-start | bytes 1769472 | tf_op jit(solution)/shard_map/all_gather | solution.py:29
  8.4 10.8 %collective-permute-start = (bf16[1,3,48,768]{3,2,1,0:T(8,128)(2,1)S(1)}, bf16[1,3,48,768]{3,2,1,0:T(8,128)(2,1)S(1)}, u32[]{:S(2)}, u32[]{:S(2)}) collective-permute-start(bf16[1,3,48,768]{3,2,1,0:T(8,128)(2,1)S(1)} %get-tuple-element.132), channel_id=1, source_target_pairs={{0,2},{2,4},{4,6},{1,3},{3,5},{5,7},{8,10},{10,12},{12,14},{9,11},... | collective-permute-start | bytes 663560 | tf_op jit(solution)/shard_map/ppermute | solution.py:16
  13.3 8.8 %collective-permute-start.1 = (bf16[1,3,48,768]{3,2,1,0:T(8,128)(2,1)S(1)}, bf16[1,3,48,768]{3,2,1,0:T(8,128)(2,1)S(1)}, u32[]{:S(2)}, u32[]{:S(2)}) collective-permute-start(bf16[1,3,48,768]{3,2,1,0:T(8,128)(2,1)S(1)} %get-tuple-element.133), channel_id=1, source_target_pairs={{2,0},{4,2},{6,4},{3,1},{5,3},{7,5},{10,8},{12,10},{14,12},{11,9},... | collective-permute-start | bytes 663560 | tf_op jit(solution)/shard_map/ppermute | solution.py:19
  45.4 24.2 %copy-start.10 = (f32[3072]{0:T(1024)S(1)}, f32[3072]{0:T(1024)}, u32[]{:S(2)}) copy-start(f32[3072]{0:T(1024)} %param.17) | copy-start | bytes 36868
  46.5 84.2 %reduce-scatter.7.cloned.1.call-start = ((), (), s32[]{:S(2)}) async-start(), calls=%async_computation.5 | async-start | bytes 3538944 | tf_op jit(solution)/shard_map/reduce_scatter | solution.py:37
  86.6 1.4 copy-start.3
  95.7 35.0 %copy-start.8 = (f32[768]{0:T(1024)S(1)}, f32[768]{0:T(1024)}, u32[]{:S(2)}) copy-start(f32[768]{0:T(1024)} %param.20) | copy-start | bytes 9220
  95.7 35.0 %copy-start.9 = (f32[768]{0:T(1024)S(1)}, f32[768]{0:T(1024)}, u32[]{:S(2)}) copy-start(f32[768]{0:T(1024)} %param.19) | copy-start | bytes 9220
  95.7 60.8 %all-gather.7.cloned.1.call-start = ((), (), s32[]{:S(2)}) async-start(), calls=%async_computation.6 | async-start | bytes 1769472 | tf_op jit(solution)/shard_map/all_gather | solution.py:29
  133.6 75.4 %reduce-scatter.9.cloned.1.call-start = ((), (), s32[]{:S(2)}) async-start(), calls=%async_computation.7 | async-start | bytes 3538944 | tf_op jit(solution)/shard_map/reduce_scatter | solution.py:37
  164.8 1.4 copy-start.5
  174.1 233.5 %reduce-scatter.11.cloned.1.call-start = ((), (), s32[]{:S(2)}) async-start(), calls=%async_computation.9 | async-start | bytes 20054016 | tf_op jit(solution)/shard_map/reduce_scatter | solution.py:41
  174.1 11.3 %copy-start.4 = (bf16[384,3072]{1,0:T(8,128)(2,1)S(1)}, bf16[384,3072]{1,0:T(8,128)(2,1)}, u32[]{:S(2)}) copy-start(bf16[384,3072]{1,0:T(8,128)(2,1)} %copy-done.3) | copy-start | bytes 7077892
  174.1 11.3 %copy-start.7 = (bf16[384,1536]{1,0:T(8,128)(2,1)S(1)}, bf16[384,1536]{1,0:T(8,128)(2,1)}, u32[]{:S(2)}) copy-start(bf16[384,1536]{1,0:T(8,128)(2,1)} %all-gather.7.cloned.1.call-done) | copy-start | bytes 3538948
  209.0 409.0 %reduce-scatter.13.cloned.1.call-start = ((), (), s32[]{:S(2)}) async-start(), calls=%async_computation.11 | async-start | bytes 21725184
  217.6 5.2 copy-start
  264.7 436.2 %all-gather.11.cloned.1.call-start = ((), (), s32[]{:S(2)}) async-start(), calls=%async_computation.10 | async-start | bytes 10027008 | tf_op jit(solution)/shard_map/all_gather | solution.py:42
  409.8 210.5 %copy-start.1 = (bf16[384,768]{1,0:T(8,128)(2,1)S(1)}, bf16[384,768]{1,0:T(8,128)(2,1)}, u32[]{:S(2)}) copy-start(bf16[384,768]{1,0:T(8,128)(2,1)} %copy-done) | copy-start | bytes 1769476
  409.8 378.4 %all-gather.9.cloned.1.call-start = ((), (), s32[]{:S(2)}) async-start(), calls=%async_computation.8 | async-start | bytes 10862592 | tf_op jit(solution)/shard_map/all_gather | solution.py:42
  620.3 6.3 collective-permute-start.2
  622.4 9.7 %copy-start.6 = (bf16[1,8,48,768]{3,2,1,0:T(8,128)(2,1)S(1)}, bf16[1,8,48,768]{3,2,1,0:T(8,128)(2,1)}, u32[]{:S(2)}) copy-start(bf16[1,8,48,768]{3,2,1,0:T(8,128)(2,1)} %param.21) | copy-start | bytes 1769476
  622.4 9.5 %collective-permute-start.3 = (bf16[1,3,48,768]{3,2,1,0:T(8,128)(2,1)S(1)}, bf16[1,3,48,768]{3,2,1,0:T(8,128)(2,1)S(1)}, u32[]{:S(2)}, u32[]{:S(2)}) collective-permute-start(bf16[1,3,48,768]{3,2,1,0:T(8,128)(2,1)S(1)} %get-tuple-element.131), channel_id=1, source_target_pairs={{2,0},{4,2},{6,4},{3,1},{5,3},{7,5},{10,8},{12,10},{14,12},{11,9},... | collective-permute-start | bytes 663560 | tf_op jit(solution)/shard_map/ppermute | solution.py:19
Sparse Core Ops, SparseCore 0:
  46.6 22.9 all-gather.4
  95.9 34.7 reduce-scatter.6
  133.7 22.7 all-gather.6
  174.2 34.7 reduce-scatter.8
  213.5 194.0 reduce-scatter.10
  411.7 206.2 reduce-scatter.12
  620.9 79.9 all-gather.10
  703.8 84.2 all-gather.8
